TPU v7x, 32 devices: a whole 2x2x4 slice. The times are simulated.
32 devices in a mesh: pp: 4 (over z), ep: 8 (over y, x, core).
Axes of the slice: x: 2, y: 2, z: 4, core: 2. Of those that a mesh axis runs over, the one named last changes fastest.
Arguments:
- inputs: bfloat16 [4, 128, 7168], P(None, 'ep'), may hold values from -16 to 16
- norm_gain: float32 [4, 7168], P('pp'), may hold values from 0.25 to 1.75
- router_weight: bfloat16 [4, 7168, 4], P('pp'), may hold values from -0.0625 to 0.0625
- gate_weight: bfloat16 [4, 7168, 4096], P('pp', None, 'ep'), may hold values from -0.0625 to 0.0625
- up_weight: bfloat16 [4, 7168, 4096], P('pp', None, 'ep'), may hold values from -0.0625 to 0.0625
- down_weight: bfloat16 [4, 1024, 28672], P('pp', None, 'ep'), may hold values from -0.1875 to 0.1875
- routing: int32 [4, 4, 128, 2], P('pp', None, 'ep'), may hold values from 0 to 3, all different within a row; in each aligned block of 16 rows (0 to 15, 16 to 31, ..., all dimensions but the last counted through in order) at most 10 rows name the same one
Outputs:
- final: bfloat16 [4, 128, 7168], P('pp', 'ep')
Inputs may be any that keep to these rules, and one draw needn't show every extreme that they name: `routing`: each token names 2 different experts. Among the 16 tokens of one device in one micro-batch of one layer, no expert is named more than 10 times, and in some of these aligned blocks one expert is named exactly 10 times.
All inputs are finite; a program needn't handle non-finite values.
Results may differ from a plain program's by a relative error of at most 0.025.
Values may be sent and summed in bfloat16 or wider, within the bound.
A program may use at most 128 MiB of HBM per device.

v0:
```python
import jax
import jax.numpy as jnp
from jax import lax
from jax.sharding import PartitionSpec as P

routed_scale = 2.5
norm_epsilon = 1e-06


def from_partner(array, axis, apart):
    return lax.ppermute(array, axis, [(i, i ^ 1 << apart) for i in range(lax.axis_size(axis))])


def from_behind(value, axis, steps):
    count = lax.axis_size(axis)
    first, last = (max(0, -steps), min(count, count - steps))
    return lax.ppermute(value, axis, [(source, source + steps) for source in range(first, last)])


def expert_rows(received, gate_block, up_block, down_block):
    member_bit = lax.axis_index("ep") % 2
    gate_proj = jnp.einsum("smd,dh->smh", received, gate_block, preferred_element_type=jnp.float32)
    up_proj = jnp.einsum("smd,dh->smh", received, up_block, preferred_element_type=jnp.float32)
    hidden = (jax.nn.silu(gate_proj) * up_proj).astype(jnp.bfloat16)
    partner = from_partner(hidden, "ep", 0)
    lower_half = jnp.where(member_bit == 0, hidden, partner)
    upper_half = jnp.where(member_bit == 0, partner, hidden)
    whole_hidden = jnp.concatenate([lower_half, upper_half], axis=2)
    outcome = jnp.einsum(
        "smh,hd->smd", whole_hidden, down_block, preferred_element_type=jnp.float32
    ).astype(jnp.bfloat16)
    return lax.all_to_all(outcome, "ep", split_axis=0, concat_axis=0, tiled=True)


def moe_layer(
    activations, micro, norm_gain, router_weight, gate_block, up_block, down_block, routing
):
    tok_rows, width = activations.shape
    experts = router_weight.shape[2]
    top_count = routing.shape[3]
    slot_count = tok_rows * top_count * 5 // (4 * experts)
    half_width = width // 2
    current = activations.astype(jnp.float32)
    mean_square = jnp.mean(current * current, axis=1, keepdims=True)
    normed = (current * lax.rsqrt(mean_square + norm_epsilon) * norm_gain[0]).astype(jnp.bfloat16)
    scores = jax.nn.sigmoid(jnp.dot(normed, router_weight[0], preferred_element_type=jnp.float32))
    routes = lax.dynamic_index_in_dim(routing[0], micro, 0, keepdims=False)
    expert_ids = jnp.arange(experts, dtype=jnp.int32)
    onehot = (routes[:, :, None] == expert_ids[None, None, :]).astype(jnp.float32)
    picked = jnp.sum(onehot * scores[:, None, :], axis=2)
    mixing = routed_scale * picked / jnp.sum(picked, axis=1, keepdims=True)
    flat_onehot = onehot.reshape(tok_rows * top_count, experts)
    earlier = jnp.cumsum(flat_onehot, axis=0) - flat_onehot
    slot_index = jnp.sum(earlier * flat_onehot, axis=1).astype(jnp.int32)
    expert_of = routes.reshape(-1)
    destination = expert_of * slot_count + slot_index
    slot_ids = jnp.arange(experts * slot_count, dtype=jnp.int32)
    targets = (destination[:, None] == slot_ids[None, :]).astype(jnp.bfloat16)
    row_owner = jnp.arange(tok_rows * top_count, dtype=jnp.int32) // top_count
    owners = (row_owner[:, None] == jnp.arange(tok_rows, dtype=jnp.int32)[None, :]).astype(
        jnp.bfloat16
    )
    selector = jnp.einsum("rs,rt->st", targets, owners, preferred_element_type=jnp.float32).astype(
        jnp.bfloat16
    )
    lower_rows = jnp.dot(
        selector, normed[:, :half_width], preferred_element_type=jnp.float32
    ).astype(jnp.bfloat16)
    upper_rows = jnp.dot(
        selector, normed[:, half_width:], preferred_element_type=jnp.float32
    ).astype(jnp.bfloat16)
    outgoing = jnp.stack(
        [
            lower_rows.reshape(experts, slot_count, half_width),
            upper_rows.reshape(experts, slot_count, half_width),
        ],
        axis=1,
    ).reshape(2 * experts, slot_count, half_width)
    received = lax.all_to_all(outgoing, "ep", split_axis=0, concat_axis=0, tiled=True)
    member_bit = lax.axis_index("ep") % 2
    partner = from_partner(received, "ep", 0)
    lower_part = jnp.where(member_bit == 0, received, partner)
    upper_part = jnp.where(member_bit == 0, partner, received)
    full_rows = jnp.concatenate([lower_part, upper_part], axis=2)
    returned = expert_rows(full_rows, gate_block, up_block, down_block)
    halves = returned.reshape(experts, 2, slot_count, half_width)
    picks = halves[expert_of, :, slot_index, :].reshape(tok_rows, top_count, width)
    combined = jnp.sum(mixing[:, :, None] * picks.astype(jnp.float32), axis=1)
    return (current + combined).astype(jnp.bfloat16)


def on_device(inputs, norm_gain, router_weight, gate_weight, up_weight, down_weight, routing):
    section_count = lax.axis_size("pp")
    section_index = lax.axis_index("pp")
    tok_rows = inputs.shape[1]
    width = inputs.shape[2]

    def advance(step_index, state):
        carried, finished = state
        finished = from_behind(finished, "pp", -1)
        micro = step_index - section_index
        is_live = jnp.logical_and(micro >= 0, micro < section_count)
        micro_safe = jnp.clip(micro, 0, section_count - 1)
        fresh_rows = lax.dynamic_index_in_dim(
            inputs, jnp.minimum(step_index, section_count - 1), 0, keepdims=False
        )
        current = jnp.where(section_index == 0, fresh_rows, carried)
        updated = moe_layer(
            current,
            micro_safe,
            norm_gain,
            router_weight,
            gate_weight[0],
            up_weight[0],
            down_weight[0],
            routing,
        )
        is_final = jnp.logical_and(section_index == section_count - 1, is_live)
        finished = jnp.where(is_final, updated[None], finished)
        carried = from_behind(updated, "pp", 1)
        return (carried, finished)

    start = (
        jnp.zeros((tok_rows, width), jnp.bfloat16),
        jnp.zeros((1, tok_rows, width), jnp.bfloat16),
    )
    carried, finished = lax.fori_loop(0, 2 * section_count - 1, advance, start)
    return finished


def solution(mesh):
    return jax.shard_map(
        on_device,
        mesh=mesh,
        in_specs=(
            P(None, "ep", None),
            P("pp", None),
            P("pp", None, None),
            P("pp", None, "ep"),
            P("pp", None, "ep"),
            P("pp", None, "ep"),
            P("pp", None, "ep", None),
        ),
        out_specs=P("pp", "ep", None),
        check_vma=False,
    )
```

profile of v0, /device:TPU:26, one launch (start us, length us, event | category | flops | bytes accessed | tf_op | source)
XLA Modules:
  0.0 473.6 jit_solution(16076083645195631959)
XLA Ops:
  0.0 472.9 %while.18 = (s32[]{:T(128)}, bf16[16,7168]{1,0:T(8,128)(2,1)S(1)}, bf16[1,16,7168]{2,1,0:T(8,128)(2,1)S(1)}, pred[]{:T(512)}, bf16[4,16,7168]{2,1,0:T(8,128)(2,1...) while((s32[]{:T(128)}, bf16[16,7168]{1,0:T(8,128)(2,1)S(1)}, ...), condition=%wide.region_7.8_spmd.clone, body=%wide.region_0.7_spmd.clone.sunk | while | flops 1780261376 | bytes 73126640 | solution.py:127
  9.6 12.5 %all-to-all-done = bf16[8,10,3584]{2,1,0:T(8,128)(2,1)S(1)} async-done(((bf16[8,10,3584]{2,1,0:T(8,128)(2,1)}), bf16[8,10,3584]{2,1,0:T(8,128)(2,1)S(1)}, u32[]{:S(2)}, u32[]{:S(2)}) %all-to-all-start) | async-done | bytes 573472 | tf_op jit(solution)/shard_map/while/body/eval_jaxpr/all_to_all | solution.py:79
  37.6 4.9 %all-to-all-start.1 = ((bf16[8,10,3584]{2,1,0:T(8,128)(2,1)}), bf16[8,10,3584]{2,1,0:T(8,128)(2,1)S(1)}, u32[]{:S(2)}, u32[]{:S(2)}) async-start(bf16[8,10,3584]{2,1,0:T(8,128)(2,1)} %fusion.73), calls=%async_computation.1 | async-start | bytes 1835008 | tf_op jit(solution)/shard_map/while/body/eval_jaxpr/all_to_all | solution.py:32
  42.7 12.3 %all-to-all-done.1 = bf16[8,10,3584]{2,1,0:T(8,128)(2,1)S(1)} async-done(((bf16[8,10,3584]{2,1,0:T(8,128)(2,1)}), bf16[8,10,3584]{2,1,0:T(8,128)(2,1)S(1)}, u32[]{:S(2)}, u32[]{:S(2)}) %all-to-all-start.1) | async-done | bytes 573472 | tf_op jit(solution)/shard_map/while/body/eval_jaxpr/all_to_all | solution.py:32
  60.3 8.2 %collective-permute-done.3 = bf16[16,7168]{1,0:T(8,128)(2,1)S(1)} collective-permute-done((bf16[16,7168]{1,0:T(8,128)(2,1)S(1)}, bf16[16,7168]{1,0:T(8,128)(2,1)S(1)}, u32[]{:S(2)}, u32[]{:S(2)}) %collective-permute-start.3) | collective-permute-done | bytes 229408 | tf_op jit(solution)/shard_map/while/body/eval_jaxpr/ppermute | solution.py:17
  77.3 12.4 %all-to-all-done = bf16[8,10,3584]{2,1,0:T(8,128)(2,1)S(1)} async-done(((bf16[8,10,3584]{2,1,0:T(8,128)(2,1)}), bf16[8,10,3584]{2,1,0:T(8,128)(2,1)S(1)}, u32[]{:S(2)}, u32[]{:S(2)}) %all-to-all-start) | async-done | bytes 573472 | tf_op jit(solution)/shard_map/while/body/eval_jaxpr/all_to_all | solution.py:79
  105.2 5.0 %all-to-all-start.1 = ((bf16[8,10,3584]{2,1,0:T(8,128)(2,1)}), bf16[8,10,3584]{2,1,0:T(8,128)(2,1)S(1)}, u32[]{:S(2)}, u32[]{:S(2)}) async-start(bf16[8,10,3584]{2,1,0:T(8,128)(2,1)} %fusion.73), calls=%async_computation.1 | async-start | bytes 1835008 | tf_op jit(solution)/shard_map/while/body/eval_jaxpr/all_to_all | solution.py:32
  110.3 12.3 %all-to-all-done.1 = bf16[8,10,3584]{2,1,0:T(8,128)(2,1)S(1)} async-done(((bf16[8,10,3584]{2,1,0:T(8,128)(2,1)}), bf16[8,10,3584]{2,1,0:T(8,128)(2,1)S(1)}, u32[]{:S(2)}, u32[]{:S(2)}) %all-to-all-start.1) | async-done | bytes 573472 | tf_op jit(solution)/shard_map/while/body/eval_jaxpr/all_to_all | solution.py:32
  127.9 8.2 %collective-permute-done.3 = bf16[16,7168]{1,0:T(8,128)(2,1)S(1)} collective-permute-done((bf16[16,7168]{1,0:T(8,128)(2,1)S(1)}, bf16[16,7168]{1,0:T(8,128)(2,1)S(1)}, u32[]{:S(2)}, u32[]{:S(2)}) %collective-permute-start.3) | collective-permute-done | bytes 229408 | tf_op jit(solution)/shard_map/while/body/eval_jaxpr/ppermute | solution.py:17
  144.9 12.4 %all-to-all-done = bf16[8,10,3584]{2,1,0:T(8,128)(2,1)S(1)} async-done(((bf16[8,10,3584]{2,1,0:T(8,128)(2,1)}), bf16[8,10,3584]{2,1,0:T(8,128)(2,1)S(1)}, u32[]{:S(2)}, u32[]{:S(2)}) %all-to-all-start) | async-done | bytes 573472 | tf_op jit(solution)/shard_map/while/body/eval_jaxpr/all_to_all | solution.py:79
  160.6 4.4 fusion.72
  172.8 5.0 %all-to-all-start.1 = ((bf16[8,10,3584]{2,1,0:T(8,128)(2,1)}), bf16[8,10,3584]{2,1,0:T(8,128)(2,1)S(1)}, u32[]{:S(2)}, u32[]{:S(2)}) async-start(bf16[8,10,3584]{2,1,0:T(8,128)(2,1)} %fusion.73), calls=%async_computation.1 | async-start | bytes 1835008 | tf_op jit(solution)/shard_map/while/body/eval_jaxpr/all_to_all | solution.py:32
  178.0 12.3 %all-to-all-done.1 = bf16[8,10,3584]{2,1,0:T(8,128)(2,1)S(1)} async-done(((bf16[8,10,3584]{2,1,0:T(8,128)(2,1)}), bf16[8,10,3584]{2,1,0:T(8,128)(2,1)S(1)}, u32[]{:S(2)}, u32[]{:S(2)}) %all-to-all-start.1) | async-done | bytes 573472 | tf_op jit(solution)/shard_map/while/body/eval_jaxpr/all_to_all | solution.py:32
  195.5 8.2 %collective-permute-done.3 = bf16[16,7168]{1,0:T(8,128)(2,1)S(1)} collective-permute-done((bf16[16,7168]{1,0:T(8,128)(2,1)S(1)}, bf16[16,7168]{1,0:T(8,128)(2,1)S(1)}, u32[]{:S(2)}, u32[]{:S(2)}) %collective-permute-start.3) | collective-permute-done | bytes 229408 | tf_op jit(solution)/shard_map/while/body/eval_jaxpr/ppermute | solution.py:17
  212.5 12.4 %all-to-all-done = bf16[8,10,3584]{2,1,0:T(8,128)(2,1)S(1)} async-done(((bf16[8,10,3584]{2,1,0:T(8,128)(2,1)}), bf16[8,10,3584]{2,1,0:T(8,128)(2,1)S(1)}, u32[]{:S(2)}, u32[]{:S(2)}) %all-to-all-start) | async-done | bytes 573472 | tf_op jit(solution)/shard_map/while/body/eval_jaxpr/all_to_all | solution.py:79
  228.0 4.4 fusion.72
  240.1 5.0 %all-to-all-start.1 = ((bf16[8,10,3584]{2,1,0:T(8,128)(2,1)}), bf16[8,10,3584]{2,1,0:T(8,128)(2,1)S(1)}, u32[]{:S(2)}, u32[]{:S(2)}) async-start(bf16[8,10,3584]{2,1,0:T(8,128)(2,1)} %fusion.73), calls=%async_computation.1 | async-start | bytes 1835008 | tf_op jit(solution)/shard_map/while/body/eval_jaxpr/all_to_all | solution.py:32
  245.3 12.3 %all-to-all-done.1 = bf16[8,10,3584]{2,1,0:T(8,128)(2,1)S(1)} async-done(((bf16[8,10,3584]{2,1,0:T(8,128)(2,1)}), bf16[8,10,3584]{2,1,0:T(8,128)(2,1)S(1)}, u32[]{:S(2)}, u32[]{:S(2)}) %all-to-all-start.1) | async-done | bytes 573472 | tf_op jit(solution)/shard_map/while/body/eval_jaxpr/all_to_all | solution.py:32
  262.9 8.2 %collective-permute-done.3 = bf16[16,7168]{1,0:T(8,128)(2,1)S(1)} collective-permute-done((bf16[16,7168]{1,0:T(8,128)(2,1)S(1)}, bf16[16,7168]{1,0:T(8,128)(2,1)S(1)}, u32[]{:S(2)}, u32[]{:S(2)}) %collective-permute-start.3) | collective-permute-done | bytes 229408 | tf_op jit(solution)/shard_map/while/body/eval_jaxpr/ppermute | solution.py:17
  279.9 12.4 %all-to-all-done = bf16[8,10,3584]{2,1,0:T(8,128)(2,1)S(1)} async-done(((bf16[8,10,3584]{2,1,0:T(8,128)(2,1)}), bf16[8,10,3584]{2,1,0:T(8,128)(2,1)S(1)}, u32[]{:S(2)}, u32[]{:S(2)}) %all-to-all-start) | async-done | bytes 573472 | tf_op jit(solution)/shard_map/while/body/eval_jaxpr/all_to_all | solution.py:79
  307.4 5.0 %all-to-all-start.1 = ((bf16[8,10,3584]{2,1,0:T(8,128)(2,1)}), bf16[8,10,3584]{2,1,0:T(8,128)(2,1)S(1)}, u32[]{:S(2)}, u32[]{:S(2)}) async-start(bf16[8,10,3584]{2,1,0:T(8,128)(2,1)} %fusion.73), calls=%async_computation.1 | async-start | bytes 1835008 | tf_op jit(solution)/shard_map/while/body/eval_jaxpr/all_to_all | solution.py:32
  312.6 12.3 %all-to-all-done.1 = bf16[8,10,3584]{2,1,0:T(8,128)(2,1)S(1)} async-done(((bf16[8,10,3584]{2,1,0:T(8,128)(2,1)}), bf16[8,10,3584]{2,1,0:T(8,128)(2,1)S(1)}, u32[]{:S(2)}, u32[]{:S(2)}) %all-to-all-start.1) | async-done | bytes 573472 | tf_op jit(solution)/shard_map/while/body/eval_jaxpr/all_to_all | solution.py:32
  330.2 8.2 %collective-permute-done.3 = bf16[16,7168]{1,0:T(8,128)(2,1)S(1)} collective-permute-done((bf16[16,7168]{1,0:T(8,128)(2,1)S(1)}, bf16[16,7168]{1,0:T(8,128)(2,1)S(1)}, u32[]{:S(2)}, u32[]{:S(2)}) %collective-permute-start.3) | collective-permute-done | bytes 229408 | tf_op jit(solution)/shard_map/while/body/eval_jaxpr/ppermute | solution.py:17
  347.2 12.4 %all-to-all-done = bf16[8,10,3584]{2,1,0:T(8,128)(2,1)S(1)} async-done(((bf16[8,10,3584]{2,1,0:T(8,128)(2,1)}), bf16[8,10,3584]{2,1,0:T(8,128)(2,1)S(1)}, u32[]{:S(2)}, u32[]{:S(2)}) %all-to-all-start) | async-done | bytes 573472 | tf_op jit(solution)/shard_map/while/body/eval_jaxpr/all_to_all | solution.py:79
  374.7 5.0 %all-to-all-start.1 = ((bf16[8,10,3584]{2,1,0:T(8,128)(2,1)}), bf16[8,10,3584]{2,1,0:T(8,128)(2,1)S(1)}, u32[]{:S(2)}, u32[]{:S(2)}) async-start(bf16[8,10,3584]{2,1,0:T(8,128)(2,1)} %fusion.73), calls=%async_computation.1 | async-start | bytes 1835008 | tf_op jit(solution)/shard_map/while/body/eval_jaxpr/all_to_all | solution.py:32
  379.9 12.3 %all-to-all-done.1 = bf16[8,10,3584]{2,1,0:T(8,128)(2,1)S(1)} async-done(((bf16[8,10,3584]{2,1,0:T(8,128)(2,1)}), bf16[8,10,3584]{2,1,0:T(8,128)(2,1)S(1)}, u32[]{:S(2)}, u32[]{:S(2)}) %all-to-all-start.1) | async-done | bytes 573472 | tf_op jit(solution)/shard_map/while/body/eval_jaxpr/all_to_all | solution.py:32
  397.5 8.2 %collective-permute-done.3 = bf16[16,7168]{1,0:T(8,128)(2,1)S(1)} collective-permute-done((bf16[16,7168]{1,0:T(8,128)(2,1)S(1)}, bf16[16,7168]{1,0:T(8,128)(2,1)S(1)}, u32[]{:S(2)}, u32[]{:S(2)}) %collective-permute-start.3) | collective-permute-done | bytes 229408 | tf_op jit(solution)/shard_map/while/body/eval_jaxpr/ppermute | solution.py:17
  414.5 12.4 %all-to-all-done = bf16[8,10,3584]{2,1,0:T(8,128)(2,1)S(1)} async-done(((bf16[8,10,3584]{2,1,0:T(8,128)(2,1)}), bf16[8,10,3584]{2,1,0:T(8,128)(2,1)S(1)}, u32[]{:S(2)}, u32[]{:S(2)}) %all-to-all-start) | async-done | bytes 573472 | tf_op jit(solution)/shard_map/while/body/eval_jaxpr/all_to_all | solution.py:79
  429.9 4.4 fusion.72
  442.0 5.0 %all-to-all-start.1 = ((bf16[8,10,3584]{2,1,0:T(8,128)(2,1)}), bf16[8,10,3584]{2,1,0:T(8,128)(2,1)S(1)}, u32[]{:S(2)}, u32[]{:S(2)}) async-start(bf16[8,10,3584]{2,1,0:T(8,128)(2,1)} %fusion.73), calls=%async_computation.1 | async-start | bytes 1835008 | tf_op jit(solution)/shard_map/while/body/eval_jaxpr/all_to_all | solution.py:32
  447.2 12.3 %all-to-all-done.1 = bf16[8,10,3584]{2,1,0:T(8,128)(2,1)S(1)} async-done(((bf16[8,10,3584]{2,1,0:T(8,128)(2,1)}), bf16[8,10,3584]{2,1,0:T(8,128)(2,1)S(1)}, u32[]{:S(2)}, u32[]{:S(2)}) %all-to-all-start.1) | async-done | bytes 573472 | tf_op jit(solution)/shard_map/while/body/eval_jaxpr/all_to_all | solution.py:32
  464.8 8.2 %collective-permute-done.3 = bf16[16,7168]{1,0:T(8,128)(2,1)S(1)} collective-permute-done((bf16[16,7168]{1,0:T(8,128)(2,1)S(1)}, bf16[16,7168]{1,0:T(8,128)(2,1)S(1)}, u32[]{:S(2)}, u32[]{:S(2)}) %collective-permute-start.3) | collective-permute-done | bytes 229408 | tf_op jit(solution)/shard_map/while/body/eval_jaxpr/ppermute | solution.py:17
  (358 shorter events, 194.4 us)
Async XLA Ops:
  5.4 16.7 %all-to-all-start = ((bf16[8,10,3584]{2,1,0:T(8,128)(2,1)}), bf16[8,10,3584]{2,1,0:T(8,128)(2,1)S(1)}, u32[]{:S(2)}, u32[]{:S(2)}) async-start(bf16[8,10,3584]{2,1,0:T(8,128)(2,1)} %bitcast.68), calls=%async_computation | async-start | bytes 1835008 | tf_op jit(solution)/shard_map/while/body/eval_jaxpr/all_to_all | solution.py:79
  22.4 2.7 collective-permute-start.1
  22.6 36.3 %collective-permute-start = (bf16[1,16,7168]{2,1,0:T(8,128)(2,1)S(1)}, bf16[1,16,7168]{2,1,0:T(8,128)(2,1)S(1)}, u32[]{:S(2)}, u32[]{:S(2)}) collective-permute-start(bf16[1,16,7168]{2,1,0:T(8,128)(2,1)S(1)} %broadcast_select_fusion.5), channel_id=1, source_target_pairs={{8,0},{16,8},{24,16},{9,1},{17,9},{25,17},{10,2},{18,10},{26,18},{... | collective-permute-start | bytes 688136 | tf_op jit(solution)/shard_map/while/body/eval_jaxpr/ppermute | solution.py:17
  37.6 17.4 %all-to-all-start.1 = ((bf16[8,10,3584]{2,1,0:T(8,128)(2,1)}), bf16[8,10,3584]{2,1,0:T(8,128)(2,1)S(1)}, u32[]{:S(2)}, u32[]{:S(2)}) async-start(bf16[8,10,3584]{2,1,0:T(8,128)(2,1)} %fusion.73), calls=%async_computation.1 | async-start | bytes 1835008 | tf_op jit(solution)/shard_map/while/body/eval_jaxpr/all_to_all | solution.py:32
  59.0 9.5 %collective-permute-start.3 = (bf16[16,7168]{1,0:T(8,128)(2,1)S(1)}, bf16[16,7168]{1,0:T(8,128)(2,1)S(1)}, u32[]{:S(2)}, u32[]{:S(2)}) collective-permute-start(bf16[16,7168]{1,0:T(8,128)(2,1)S(1)} %get-tuple-element.517), channel_id=1, source_target_pairs={{0,8},{8,16},{16,24},{1,9},{9,17},{17,25},{2,10},{10,18},{18,26},{... | collective-permute-start | bytes 688136 | tf_op jit(solution)/shard_map/while/body/eval_jaxpr/ppermute | solution.py:17
  73.8 15.9 %all-to-all-start = ((bf16[8,10,3584]{2,1,0:T(8,128)(2,1)}), bf16[8,10,3584]{2,1,0:T(8,128)(2,1)S(1)}, u32[]{:S(2)}, u32[]{:S(2)}) async-start(bf16[8,10,3584]{2,1,0:T(8,128)(2,1)} %bitcast.68), calls=%async_computation | async-start | bytes 1835008 | tf_op jit(solution)/shard_map/while/body/eval_jaxpr/all_to_all | solution.py:79
  90.0 2.7 collective-permute-start.1
  90.2 36.3 %collective-permute-start = (bf16[1,16,7168]{2,1,0:T(8,128)(2,1)S(1)}, bf16[1,16,7168]{2,1,0:T(8,128)(2,1)S(1)}, u32[]{:S(2)}, u32[]{:S(2)}) collective-permute-start(bf16[1,16,7168]{2,1,0:T(8,128)(2,1)S(1)} %broadcast_select_fusion.5), channel_id=1, source_target_pairs={{8,0},{16,8},{24,16},{9,1},{17,9},{25,17},{10,2},{18,10},{26,18},{... | collective-permute-start | bytes 688136 | tf_op jit(solution)/shard_map/while/body/eval_jaxpr/ppermute | solution.py:17
  105.2 17.4 %all-to-all-start.1 = ((bf16[8,10,3584]{2,1,0:T(8,128)(2,1)}), bf16[8,10,3584]{2,1,0:T(8,128)(2,1)S(1)}, u32[]{:S(2)}, u32[]{:S(2)}) async-start(bf16[8,10,3584]{2,1,0:T(8,128)(2,1)} %fusion.73), calls=%async_computation.1 | async-start | bytes 1835008 | tf_op jit(solution)/shard_map/while/body/eval_jaxpr/all_to_all | solution.py:32
  126.6 9.5 %collective-permute-start.3 = (bf16[16,7168]{1,0:T(8,128)(2,1)S(1)}, bf16[16,7168]{1,0:T(8,128)(2,1)S(1)}, u32[]{:S(2)}, u32[]{:S(2)}) collective-permute-start(bf16[16,7168]{1,0:T(8,128)(2,1)S(1)} %get-tuple-element.517), channel_id=1, source_target_pairs={{0,8},{8,16},{16,24},{1,9},{9,17},{17,25},{2,10},{10,18},{18,26},{... | collective-permute-start | bytes 688136 | tf_op jit(solution)/shard_map/while/body/eval_jaxpr/ppermute | solution.py:17
  141.4 15.9 %all-to-all-start = ((bf16[8,10,3584]{2,1,0:T(8,128)(2,1)}), bf16[8,10,3584]{2,1,0:T(8,128)(2,1)S(1)}, u32[]{:S(2)}, u32[]{:S(2)}) async-start(bf16[8,10,3584]{2,1,0:T(8,128)(2,1)} %bitcast.68), calls=%async_computation | async-start | bytes 1835008 | tf_op jit(solution)/shard_map/while/body/eval_jaxpr/all_to_all | solution.py:79
  157.6 2.7 collective-permute-start.1
  157.8 36.3 %collective-permute-start = (bf16[1,16,7168]{2,1,0:T(8,128)(2,1)S(1)}, bf16[1,16,7168]{2,1,0:T(8,128)(2,1)S(1)}, u32[]{:S(2)}, u32[]{:S(2)}) collective-permute-start(bf16[1,16,7168]{2,1,0:T(8,128)(2,1)S(1)} %broadcast_select_fusion.5), channel_id=1, source_target_pairs={{8,0},{16,8},{24,16},{9,1},{17,9},{25,17},{10,2},{18,10},{26,18},{... | collective-permute-start | bytes 688136 | tf_op jit(solution)/shard_map/while/body/eval_jaxpr/ppermute | solution.py:17
  172.8 17.4 %all-to-all-start.1 = ((bf16[8,10,3584]{2,1,0:T(8,128)(2,1)}), bf16[8,10,3584]{2,1,0:T(8,128)(2,1)S(1)}, u32[]{:S(2)}, u32[]{:S(2)}) async-start(bf16[8,10,3584]{2,1,0:T(8,128)(2,1)} %fusion.73), calls=%async_computation.1 | async-start | bytes 1835008 | tf_op jit(solution)/shard_map/while/body/eval_jaxpr/all_to_all | solution.py:32
  194.2 9.5 %collective-permute-start.3 = (bf16[16,7168]{1,0:T(8,128)(2,1)S(1)}, bf16[16,7168]{1,0:T(8,128)(2,1)S(1)}, u32[]{:S(2)}, u32[]{:S(2)}) collective-permute-start(bf16[16,7168]{1,0:T(8,128)(2,1)S(1)} %get-tuple-element.517), channel_id=1, source_target_pairs={{0,8},{8,16},{16,24},{1,9},{9,17},{17,25},{2,10},{10,18},{18,26},{... | collective-permute-start | bytes 688136 | tf_op jit(solution)/shard_map/while/body/eval_jaxpr/ppermute | solution.py:17
  209.0 15.9 %all-to-all-start = ((bf16[8,10,3584]{2,1,0:T(8,128)(2,1)}), bf16[8,10,3584]{2,1,0:T(8,128)(2,1)S(1)}, u32[]{:S(2)}, u32[]{:S(2)}) async-start(bf16[8,10,3584]{2,1,0:T(8,128)(2,1)} %bitcast.68), calls=%async_computation | async-start | bytes 1835008 | tf_op jit(solution)/shard_map/while/body/eval_jaxpr/all_to_all | solution.py:79
  225.3 2.4 collective-permute-start.1
  225.4 36.0 %collective-permute-start = (bf16[1,16,7168]{2,1,0:T(8,128)(2,1)S(1)}, bf16[1,16,7168]{2,1,0:T(8,128)(2,1)S(1)}, u32[]{:S(2)}, u32[]{:S(2)}) collective-permute-start(bf16[1,16,7168]{2,1,0:T(8,128)(2,1)S(1)} %broadcast_select_fusion.5), channel_id=1, source_target_pairs={{8,0},{16,8},{24,16},{9,1},{17,9},{25,17},{10,2},{18,10},{26,18},{... | collective-permute-start | bytes 688136 | tf_op jit(solution)/shard_map/while/body/eval_jaxpr/ppermute | solution.py:17
  240.1 17.4 %all-to-all-start.1 = ((bf16[8,10,3584]{2,1,0:T(8,128)(2,1)}), bf16[8,10,3584]{2,1,0:T(8,128)(2,1)S(1)}, u32[]{:S(2)}, u32[]{:S(2)}) async-start(bf16[8,10,3584]{2,1,0:T(8,128)(2,1)} %fusion.73), calls=%async_computation.1 | async-start | bytes 1835008 | tf_op jit(solution)/shard_map/while/body/eval_jaxpr/all_to_all | solution.py:32
  261.6 9.5 %collective-permute-start.3 = (bf16[16,7168]{1,0:T(8,128)(2,1)S(1)}, bf16[16,7168]{1,0:T(8,128)(2,1)S(1)}, u32[]{:S(2)}, u32[]{:S(2)}) collective-permute-start(bf16[16,7168]{1,0:T(8,128)(2,1)S(1)} %get-tuple-element.517), channel_id=1, source_target_pairs={{0,8},{8,16},{16,24},{1,9},{9,17},{17,25},{2,10},{10,18},{18,26},{... | collective-permute-start | bytes 688136 | tf_op jit(solution)/shard_map/while/body/eval_jaxpr/ppermute | solution.py:17
  276.3 15.9 %all-to-all-start = ((bf16[8,10,3584]{2,1,0:T(8,128)(2,1)}), bf16[8,10,3584]{2,1,0:T(8,128)(2,1)S(1)}, u32[]{:S(2)}, u32[]{:S(2)}) async-start(bf16[8,10,3584]{2,1,0:T(8,128)(2,1)} %bitcast.68), calls=%async_computation | async-start | bytes 1835008 | tf_op jit(solution)/shard_map/while/body/eval_jaxpr/all_to_all | solution.py:79
  292.7 36.0 %collective-permute-start = (bf16[1,16,7168]{2,1,0:T(8,128)(2,1)S(1)}, bf16[1,16,7168]{2,1,0:T(8,128)(2,1)S(1)}, u32[]{:S(2)}, u32[]{:S(2)}) collective-permute-start(bf16[1,16,7168]{2,1,0:T(8,128)(2,1)S(1)} %broadcast_select_fusion.5), channel_id=1, source_target_pairs={{8,0},{16,8},{24,16},{9,1},{17,9},{25,17},{10,2},{18,10},{26,18},{... | collective-permute-start | bytes 688136 | tf_op jit(solution)/shard_map/while/body/eval_jaxpr/ppermute | solution.py:17
  307.4 17.4 %all-to-all-start.1 = ((bf16[8,10,3584]{2,1,0:T(8,128)(2,1)}), bf16[8,10,3584]{2,1,0:T(8,128)(2,1)S(1)}, u32[]{:S(2)}, u32[]{:S(2)}) async-start(bf16[8,10,3584]{2,1,0:T(8,128)(2,1)} %fusion.73), calls=%async_computation.1 | async-start | bytes 1835008 | tf_op jit(solution)/shard_map/while/body/eval_jaxpr/all_to_all | solution.py:32
  328.9 9.5 %collective-permute-start.3 = (bf16[16,7168]{1,0:T(8,128)(2,1)S(1)}, bf16[16,7168]{1,0:T(8,128)(2,1)S(1)}, u32[]{:S(2)}, u32[]{:S(2)}) collective-permute-start(bf16[16,7168]{1,0:T(8,128)(2,1)S(1)} %get-tuple-element.517), channel_id=1, source_target_pairs={{0,8},{8,16},{16,24},{1,9},{9,17},{17,25},{2,10},{10,18},{18,26},{... | collective-permute-start | bytes 688136 | tf_op jit(solution)/shard_map/while/body/eval_jaxpr/ppermute | solution.py:17
  343.6 15.9 %all-to-all-start = ((bf16[8,10,3584]{2,1,0:T(8,128)(2,1)}), bf16[8,10,3584]{2,1,0:T(8,128)(2,1)S(1)}, u32[]{:S(2)}, u32[]{:S(2)}) async-start(bf16[8,10,3584]{2,1,0:T(8,128)(2,1)} %bitcast.68), calls=%async_computation | async-start | bytes 1835008 | tf_op jit(solution)/shard_map/while/body/eval_jaxpr/all_to_all | solution.py:79
  360.0 36.0 %collective-permute-start = (bf16[1,16,7168]{2,1,0:T(8,128)(2,1)S(1)}, bf16[1,16,7168]{2,1,0:T(8,128)(2,1)S(1)}, u32[]{:S(2)}, u32[]{:S(2)}) collective-permute-start(bf16[1,16,7168]{2,1,0:T(8,128)(2,1)S(1)} %broadcast_select_fusion.5), channel_id=1, source_target_pairs={{8,0},{16,8},{24,16},{9,1},{17,9},{25,17},{10,2},{18,10},{26,18},{... | collective-permute-start | bytes 688136 | tf_op jit(solution)/shard_map/while/body/eval_jaxpr/ppermute | solution.py:17
  374.7 17.4 %all-to-all-start.1 = ((bf16[8,10,3584]{2,1,0:T(8,128)(2,1)}), bf16[8,10,3584]{2,1,0:T(8,128)(2,1)S(1)}, u32[]{:S(2)}, u32[]{:S(2)}) async-start(bf16[8,10,3584]{2,1,0:T(8,128)(2,1)} %fusion.73), calls=%async_computation.1 | async-start | bytes 1835008 | tf_op jit(solution)/shard_map/while/body/eval_jaxpr/all_to_all | solution.py:32
  396.2 9.5 %collective-permute-start.3 = (bf16[16,7168]{1,0:T(8,128)(2,1)S(1)}, bf16[16,7168]{1,0:T(8,128)(2,1)S(1)}, u32[]{:S(2)}, u32[]{:S(2)}) collective-permute-start(bf16[16,7168]{1,0:T(8,128)(2,1)S(1)} %get-tuple-element.517), channel_id=1, source_target_pairs={{0,8},{8,16},{16,24},{1,9},{9,17},{17,25},{2,10},{10,18},{18,26},{... | collective-permute-start | bytes 688136 | tf_op jit(solution)/shard_map/while/body/eval_jaxpr/ppermute | solution.py:17
  411.0 15.9 %all-to-all-start = ((bf16[8,10,3584]{2,1,0:T(8,128)(2,1)}), bf16[8,10,3584]{2,1,0:T(8,128)(2,1)S(1)}, u32[]{:S(2)}, u32[]{:S(2)}) async-start(bf16[8,10,3584]{2,1,0:T(8,128)(2,1)} %bitcast.68), calls=%async_computation | async-start | bytes 1835008 | tf_op jit(solution)/shard_map/while/body/eval_jaxpr/all_to_all | solution.py:79
  427.3 36.0 %collective-permute-start = (bf16[1,16,7168]{2,1,0:T(8,128)(2,1)S(1)}, bf16[1,16,7168]{2,1,0:T(8,128)(2,1)S(1)}, u32[]{:S(2)}, u32[]{:S(2)}) collective-permute-start(bf16[1,16,7168]{2,1,0:T(8,128)(2,1)S(1)} %broadcast_select_fusion.5), channel_id=1, source_target_pairs={{8,0},{16,8},{24,16},{9,1},{17,9},{25,17},{10,2},{18,10},{26,18},{... | collective-permute-start | bytes 688136 | tf_op jit(solution)/shard_map/while/body/eval_jaxpr/ppermute | solution.py:17
  442.0 17.4 %all-to-all-start.1 = ((bf16[8,10,3584]{2,1,0:T(8,128)(2,1)}), bf16[8,10,3584]{2,1,0:T(8,128)(2,1)S(1)}, u32[]{:S(2)}, u32[]{:S(2)}) async-start(bf16[8,10,3584]{2,1,0:T(8,128)(2,1)} %fusion.73), calls=%async_computation.1 | async-start | bytes 1835008 | tf_op jit(solution)/shard_map/while/body/eval_jaxpr/all_to_all | solution.py:32
  463.5 9.5 %collective-permute-start.3 = (bf16[16,7168]{1,0:T(8,128)(2,1)S(1)}, bf16[16,7168]{1,0:T(8,128)(2,1)S(1)}, u32[]{:S(2)}, u32[]{:S(2)}) collective-permute-start(bf16[16,7168]{1,0:T(8,128)(2,1)S(1)} %get-tuple-element.517), channel_id=1, source_target_pairs={{0,8},{8,16},{16,24},{1,9},{9,17},{17,25},{2,10},{10,18},{18,26},{... | collective-permute-start | bytes 688136 | tf_op jit(solution)/shard_map/while/body/eval_jaxpr/ppermute | solution.py:17
  (32 other events, 299.0 us)
where the time goes:
time: 476 us; the launch traced here: 474 us
  waiting for transfers between devices  233 us (49%)
  starting transfers between devices  86.7 us (18%)
  matrix products  81.2 us (17%)
  local copies, waits for them, and re-layouts  41.9 us (9%)
  other arithmetic  28.7 us (6%)
    all_to_all x7, waiting for transfers between devices, moe_layer(): lax.all_to_all(outgoing, 'ep', split_axis=0, concat_axis=0, tiled=True)  86.9 us
    all_to_all x7, waiting for transfers between devices, expert_rows(): lax.all_to_all(outcome, 'ep', split_axis=0, concat_axis=0, tiled=True)  85.8 us
    ppermute x14, waiting for transfers between devices, from_behind(): lax.ppermute(value, axis, [(source, source + steps) for source in range(f...  57.1 us
    all_to_all x7, starting transfers between devices, expert_rows(): lax.all_to_all(outcome, 'ep', split_axis=0, concat_axis=0, tiled=True)  34.6 us
    dot_general x7, matrix products, expert_rows(): jnp.einsum('smd,dh->smh', received, gate_block, preferred_element_type=jn...  30.5 us
    dot_general x7, matrix products, expert_rows(): jnp.einsum('smd,dh->smh', received, up_block, preferred_element_type=jnp....  29.5 us
    all_to_all x7, starting transfers between devices, moe_layer(): lax.all_to_all(outgoing, 'ep', split_axis=0, concat_axis=0, tiled=True)  25.3 us
    ppermute x14, starting transfers between devices, from_behind(): lax.ppermute(value, axis, [(source, source + steps) for source in range(f...  24.3 us
  transfers between devices with their start and end apart: 42, of which 28 were waited for; matrix products, arithmetic and copies ran while one was open for 23% of the time, Pallas kernels for 0%

commit v1 on v0

--- a/solution.py
+++ b/solution.py
@@ -76,7 +76,15 @@
         ],
         axis=1,
     ).reshape(2 * experts, slot_count, half_width)
-    received = lax.all_to_all(outgoing, "ep", split_axis=0, concat_axis=0, tiled=True)
+    ways, here = (lax.axis_size("ep"), lax.axis_index("ep"))
+    width_2 = outgoing.shape[0] // ways
+    turned = jnp.roll(outgoing, -here * width_2, axis=0)
+    got = [lax.slice_in_dim(turned, 0, width_2, axis=0)]
+    for far in range(1, ways):
+        sent = lax.slice_in_dim(turned, far * width_2, (far + 1) * width_2, axis=0)
+        got.append(lax.ppermute(sent, "ep", [(d, (d + far) % ways) for d in range(ways)]))
+    line = jnp.concatenate(got[::-1], axis=0)
+    received = jnp.roll(line, (here + 1) * got[0].shape[0], axis=0)
     member_bit = lax.axis_index("ep") % 2
     partner = from_partner(received, "ep", 0)
     lower_part = jnp.where(member_bit == 0, received, partner)

time: 476 us -> 479 us (level)
  waiting for transfers between devices: 233 us -> 191 us
  starting transfers between devices: 86.7 us -> 101 us
  matrix products: 81.2 us -> 92.3 us
  local copies, waits for them, and re-layouts: 41.9 us -> 52.5 us
  other arithmetic: 28.7 us -> 37.4 us
    all_to_all x7 -> x0, waiting for transfers between devices: 86.9 us -> none  [moe_layer(): lax.all_to_all(outgoing, 'ep', split_axis=0, concat_axis=0, tiled=True)]
    ppermute x0 -> x49, waiting for transfers between devices: none -> 44.6 us  [moe_layer(): lax.ppermute(sent, 'ep', [(d, (d + far) % ways) for d in range(ways)])]
    ppermute x0 -> x49, starting transfers between devices: none -> 35.3 us  [moe_layer(): lax.ppermute(sent, 'ep', [(d, (d + far) % ways) for d in range(ways)])]
    all_to_all x7 -> x0, starting transfers between devices: 25.3 us -> none  [moe_layer(): lax.all_to_all(outgoing, 'ep', split_axis=0, concat_axis=0, tiled=True)]
    while x42 -> x147, local copies, waits for them, and re-layouts: 0.19 us -> 16.8 us
    dot_general x7, matrix products: 1.28 us -> 11.2 us  [moe_layer(): jnp.dot(normed, router_weight[0], preferred_element_type=jnp.float32)]
    another operation x7, local copies, waits for them, and re-layouts: 6.94 us -> 0.43 us  [moe_layer(): jnp.stack([lower_rows.reshape(experts, slot_count, half_width), upper_row...]
    concatenate x0 -> x14, other arithmetic: none -> 5.68 us  [the longest x7 2.85 us: moe_layer(): received = jnp.roll(line, (here + 1) * got[0].shape[0], axis=0)]
  transfers between devices with their start and end apart: 42 -> 84, of which waited for: 28 -> 50; matrix products, arithmetic and copies ran while one was open for 23% -> 29% of each run, Pallas kernels for 0% -> 0%
where the time goes in v1:
time: 479 us; the launch traced here: 476 us
  waiting for transfers between devices  191 us (40%)
  starting transfers between devices  101 us (21%)
  matrix products  92.3 us (19%)
  local copies, waits for them, and re-layouts  52.5 us (11%)
  other arithmetic  37.4 us (8%)
    all_to_all x7, waiting for transfers between devices, expert_rows(): lax.all_to_all(outcome, 'ep', split_axis=0, concat_axis=0, tiled=True)  85.7 us
    ppermute x14, waiting for transfers between devices, from_behind(): lax.ppermute(value, axis, [(source, source + steps) for source in range(f...  57.1 us
    ppermute x49, waiting for transfers between devices, moe_layer(): lax.ppermute(sent, 'ep', [(d, (d + far) % ways) for d in range(ways)])  44.6 us
    all_to_all x7, starting transfers between devices, expert_rows(): lax.all_to_all(outcome, 'ep', split_axis=0, concat_axis=0, tiled=True)  38.5 us
    ppermute x49, starting transfers between devices, moe_layer(): lax.ppermute(sent, 'ep', [(d, (d + far) % ways) for d in range(ways)])  35.3 us
    dot_general x7, matrix products, expert_rows(): jnp.einsum('smd,dh->smh', received, gate_block, preferred_element_type=jn...  31.7 us
    dot_general x7, matrix products, expert_rows(): jnp.einsum('smd,dh->smh', received, up_block, preferred_element_type=jnp....  29.5 us
    ppermute x14, starting transfers between devices, from_behind(): lax.ppermute(value, axis, [(source, source + steps) for source in range(f...  24.3 us
  transfers between devices with their start and end apart: 84, of which 50 were waited for; matrix products, arithmetic and copies ran while one was open for 29% of the time, Pallas kernels for 0%

profile of v1, /device:TPU:26, one launch (start us, length us, event | category | flops | bytes accessed | tf_op | source)
XLA Modules:
  0.0 476.0 jit_solution(14756149391605410866)
XLA Ops:
  0.0 475.3 %while.18 = (s32[]{:T(128)}, bf16[16,7168]{1,0:T(8,128)(2,1)S(1)}, bf16[1,16,7168]{2,1,0:T(8,128)(2,1)S(1)}, pred[]{:T(512)}, bf16[4,16,7168]{2,1,0:T(8,128)(2,1...) while((s32[]{:T(128)}, bf16[16,7168]{1,0:T(8,128)(2,1)S(1)}, ...), condition=%wide.region_7.9_spmd.clone, body=%wide.region_0.8_spmd.clone.sunk | while | flops 1781121536 | bytes 77502904 | solution.py:135
  24.9 4.5 fusion.81
  37.3 5.9 %all-to-all-start = ((bf16[8,10,3584]{2,1,0:T(8,128)(2,1)}), bf16[8,10,3584]{2,1,0:T(8,128)(2,1)S(1)}, u32[]{:S(2)}, u32[]{:S(2)}) async-start(bf16[8,10,3584]{2,1,0:T(8,128)(2,1)} %fusion.82), calls=%async_computation | async-start | bytes 1835008 | tf_op jit(solution)/shard_map/while/body/eval_jaxpr/all_to_all | solution.py:32
  43.4 12.2 %all-to-all-done = bf16[8,10,3584]{2,1,0:T(8,128)(2,1)S(1)} async-done(((bf16[8,10,3584]{2,1,0:T(8,128)(2,1)}), bf16[8,10,3584]{2,1,0:T(8,128)(2,1)S(1)}, u32[]{:S(2)}, u32[]{:S(2)}) %all-to-all-start) | async-done | bytes 573472 | tf_op jit(solution)/shard_map/while/body/eval_jaxpr/all_to_all | solution.py:32
  61.0 8.2 %collective-permute-done.10 = bf16[16,7168]{1,0:T(8,128)(2,1)S(1)} collective-permute-done((bf16[16,7168]{1,0:T(8,128)(2,1)S(1)}, bf16[16,7168]{1,0:T(8,128)(2,1)S(1)}, u32[]{:S(2)}, u32[]{:S(2)}) %collective-permute-start.10) | collective-permute-done | bytes 229408 | tf_op jit(solution)/shard_map/while/body/eval_jaxpr/ppermute | solution.py:17
  93.3 4.5 fusion.81
  97.8 4.2 multiply_convert_fusion.2
  105.6 5.4 %all-to-all-start = ((bf16[8,10,3584]{2,1,0:T(8,128)(2,1)}), bf16[8,10,3584]{2,1,0:T(8,128)(2,1)S(1)}, u32[]{:S(2)}, u32[]{:S(2)}) async-start(bf16[8,10,3584]{2,1,0:T(8,128)(2,1)} %fusion.82), calls=%async_computation | async-start | bytes 1835008 | tf_op jit(solution)/shard_map/while/body/eval_jaxpr/all_to_all | solution.py:32
  111.3 12.2 %all-to-all-done = bf16[8,10,3584]{2,1,0:T(8,128)(2,1)S(1)} async-done(((bf16[8,10,3584]{2,1,0:T(8,128)(2,1)}), bf16[8,10,3584]{2,1,0:T(8,128)(2,1)S(1)}, u32[]{:S(2)}, u32[]{:S(2)}) %all-to-all-start) | async-done | bytes 573472 | tf_op jit(solution)/shard_map/while/body/eval_jaxpr/all_to_all | solution.py:32
  128.9 8.2 %collective-permute-done.10 = bf16[16,7168]{1,0:T(8,128)(2,1)S(1)} collective-permute-done((bf16[16,7168]{1,0:T(8,128)(2,1)S(1)}, bf16[16,7168]{1,0:T(8,128)(2,1)S(1)}, u32[]{:S(2)}, u32[]{:S(2)}) %collective-permute-start.10) | collective-permute-done | bytes 229408 | tf_op jit(solution)/shard_map/while/body/eval_jaxpr/ppermute | solution.py:17
  161.2 4.5 fusion.81
  165.7 4.2 multiply_convert_fusion.2
  173.5 5.4 %all-to-all-start = ((bf16[8,10,3584]{2,1,0:T(8,128)(2,1)}), bf16[8,10,3584]{2,1,0:T(8,128)(2,1)S(1)}, u32[]{:S(2)}, u32[]{:S(2)}) async-start(bf16[8,10,3584]{2,1,0:T(8,128)(2,1)} %fusion.82), calls=%async_computation | async-start | bytes 1835008 | tf_op jit(solution)/shard_map/while/body/eval_jaxpr/all_to_all | solution.py:32
  179.2 12.2 %all-to-all-done = bf16[8,10,3584]{2,1,0:T(8,128)(2,1)S(1)} async-done(((bf16[8,10,3584]{2,1,0:T(8,128)(2,1)}), bf16[8,10,3584]{2,1,0:T(8,128)(2,1)S(1)}, u32[]{:S(2)}, u32[]{:S(2)}) %all-to-all-start) | async-done | bytes 573472 | tf_op jit(solution)/shard_map/while/body/eval_jaxpr/all_to_all | solution.py:32
  196.8 8.2 %collective-permute-done.10 = bf16[16,7168]{1,0:T(8,128)(2,1)S(1)} collective-permute-done((bf16[16,7168]{1,0:T(8,128)(2,1)S(1)}, bf16[16,7168]{1,0:T(8,128)(2,1)S(1)}, u32[]{:S(2)}, u32[]{:S(2)}) %collective-permute-start.10) | collective-permute-done | bytes 229408 | tf_op jit(solution)/shard_map/while/body/eval_jaxpr/ppermute | solution.py:17
  228.8 4.5 fusion.81
  233.3 4.2 multiply_convert_fusion.2
  241.1 5.4 %all-to-all-start = ((bf16[8,10,3584]{2,1,0:T(8,128)(2,1)}), bf16[8,10,3584]{2,1,0:T(8,128)(2,1)S(1)}, u32[]{:S(2)}, u32[]{:S(2)}) async-start(bf16[8,10,3584]{2,1,0:T(8,128)(2,1)} %fusion.82), calls=%async_computation | async-start | bytes 1835008 | tf_op jit(solution)/shard_map/while/body/eval_jaxpr/all_to_all | solution.py:32
  246.8 12.2 %all-to-all-done = bf16[8,10,3584]{2,1,0:T(8,128)(2,1)S(1)} async-done(((bf16[8,10,3584]{2,1,0:T(8,128)(2,1)}), bf16[8,10,3584]{2,1,0:T(8,128)(2,1)S(1)}, u32[]{:S(2)}, u32[]{:S(2)}) %all-to-all-start) | async-done | bytes 573472 | tf_op jit(solution)/shard_map/while/body/eval_jaxpr/all_to_all | solution.py:32
  264.4 8.2 %collective-permute-done.10 = bf16[16,7168]{1,0:T(8,128)(2,1)S(1)} collective-permute-done((bf16[16,7168]{1,0:T(8,128)(2,1)S(1)}, bf16[16,7168]{1,0:T(8,128)(2,1)S(1)}, u32[]{:S(2)}, u32[]{:S(2)}) %collective-permute-start.10) | collective-permute-done | bytes 229408 | tf_op jit(solution)/shard_map/while/body/eval_jaxpr/ppermute | solution.py:17
  296.4 4.5 fusion.81
  308.7 5.4 %all-to-all-start = ((bf16[8,10,3584]{2,1,0:T(8,128)(2,1)}), bf16[8,10,3584]{2,1,0:T(8,128)(2,1)S(1)}, u32[]{:S(2)}, u32[]{:S(2)}) async-start(bf16[8,10,3584]{2,1,0:T(8,128)(2,1)} %fusion.82), calls=%async_computation | async-start | bytes 1835008 | tf_op jit(solution)/shard_map/while/body/eval_jaxpr/all_to_all | solution.py:32
  314.4 12.2 %all-to-all-done = bf16[8,10,3584]{2,1,0:T(8,128)(2,1)S(1)} async-done(((bf16[8,10,3584]{2,1,0:T(8,128)(2,1)}), bf16[8,10,3584]{2,1,0:T(8,128)(2,1)S(1)}, u32[]{:S(2)}, u32[]{:S(2)}) %all-to-all-start) | async-done | bytes 573472 | tf_op jit(solution)/shard_map/while/body/eval_jaxpr/all_to_all | solution.py:32
  332.0 8.2 %collective-permute-done.10 = bf16[16,7168]{1,0:T(8,128)(2,1)S(1)} collective-permute-done((bf16[16,7168]{1,0:T(8,128)(2,1)S(1)}, bf16[16,7168]{1,0:T(8,128)(2,1)S(1)}, u32[]{:S(2)}, u32[]{:S(2)}) %collective-permute-start.10) | collective-permute-done | bytes 229408 | tf_op jit(solution)/shard_map/while/body/eval_jaxpr/ppermute | solution.py:17
  364.0 4.5 fusion.81
  376.3 5.5 %all-to-all-start = ((bf16[8,10,3584]{2,1,0:T(8,128)(2,1)}), bf16[8,10,3584]{2,1,0:T(8,128)(2,1)S(1)}, u32[]{:S(2)}, u32[]{:S(2)}) async-start(bf16[8,10,3584]{2,1,0:T(8,128)(2,1)} %fusion.82), calls=%async_computation | async-start | bytes 1835008 | tf_op jit(solution)/shard_map/while/body/eval_jaxpr/all_to_all | solution.py:32
  382.0 12.2 %all-to-all-done = bf16[8,10,3584]{2,1,0:T(8,128)(2,1)S(1)} async-done(((bf16[8,10,3584]{2,1,0:T(8,128)(2,1)}), bf16[8,10,3584]{2,1,0:T(8,128)(2,1)S(1)}, u32[]{:S(2)}, u32[]{:S(2)}) %all-to-all-start) | async-done | bytes 573472 | tf_op jit(solution)/shard_map/while/body/eval_jaxpr/all_to_all | solution.py:32
  399.6 8.2 %collective-permute-done.10 = bf16[16,7168]{1,0:T(8,128)(2,1)S(1)} collective-permute-done((bf16[16,7168]{1,0:T(8,128)(2,1)S(1)}, bf16[16,7168]{1,0:T(8,128)(2,1)S(1)}, u32[]{:S(2)}, u32[]{:S(2)}) %collective-permute-start.10) | collective-permute-done | bytes 229408 | tf_op jit(solution)/shard_map/while/body/eval_jaxpr/ppermute | solution.py:17
  431.6 4.5 fusion.81
  443.9 5.4 %all-to-all-start = ((bf16[8,10,3584]{2,1,0:T(8,128)(2,1)}), bf16[8,10,3584]{2,1,0:T(8,128)(2,1)S(1)}, u32[]{:S(2)}, u32[]{:S(2)}) async-start(bf16[8,10,3584]{2,1,0:T(8,128)(2,1)} %fusion.82), calls=%async_computation | async-start | bytes 1835008 | tf_op jit(solution)/shard_map/while/body/eval_jaxpr/all_to_all | solution.py:32
  449.6 12.2 %all-to-all-done = bf16[8,10,3584]{2,1,0:T(8,128)(2,1)S(1)} async-done(((bf16[8,10,3584]{2,1,0:T(8,128)(2,1)}), bf16[8,10,3584]{2,1,0:T(8,128)(2,1)S(1)}, u32[]{:S(2)}, u32[]{:S(2)}) %all-to-all-start) | async-done | bytes 573472 | tf_op jit(solution)/shard_map/while/body/eval_jaxpr/all_to_all | solution.py:32
  467.2 8.2 %collective-permute-done.10 = bf16[16,7168]{1,0:T(8,128)(2,1)S(1)} collective-permute-done((bf16[16,7168]{1,0:T(8,128)(2,1)S(1)}, bf16[16,7168]{1,0:T(8,128)(2,1)S(1)}, u32[]{:S(2)}, u32[]{:S(2)}) %collective-permute-start.10) | collective-permute-done | bytes 229408 | tf_op jit(solution)/shard_map/while/body/eval_jaxpr/ppermute | solution.py:17
  (575 shorter events, 247.6 us)
Async XLA Ops:
  8.0 11.2 %collective-permute-start.4 = (bf16[1,10,3584]{2,1,0:T(8,128)(2,1)S(1)}, bf16[1,10,3584]{2,1,0:T(8,128)(2,1)S(1)}, u32[]{:S(2)}, u32[]{:S(2)}) collective-permute-start(bf16[1,10,3584]{2,1,0:T(8,128)(2,1)S(1)} %get-tuple-element.529), channel_id=1, source_target_pairs={{0,4},{1,5},{2,6},{3,7},{4,0},{5,1},{6,2},{7,3},{8,12},{9,13},{10,... | collective-permute-start | bytes 215048 | tf_op jit(solution)/shard_map/while/body/eval_jaxpr/ppermute | solution.py:85
  8.5 10.8 %collective-permute-start.5 = (bf16[1,10,3584]{2,1,0:T(8,128)(2,1)S(1)}, bf16[1,10,3584]{2,1,0:T(8,128)(2,1)S(1)}, u32[]{:S(2)}, u32[]{:S(2)}) collective-permute-start(bf16[1,10,3584]{2,1,0:T(8,128)(2,1)S(1)} %get-tuple-element.530), channel_id=1, source_target_pairs={{0,3},{1,4},{2,5},{3,6},{4,7},{5,0},{6,1},{7,2},{8,11},{9,12},{10,... | collective-permute-start | bytes 215048 | tf_op jit(solution)/shard_map/while/body/eval_jaxpr/ppermute | solution.py:85
  20.2 39.3 %collective-permute-start = (bf16[1,16,7168]{2,1,0:T(8,128)(2,1)S(1)}, bf16[1,16,7168]{2,1,0:T(8,128)(2,1)S(1)}, u32[]{:S(2)}, u32[]{:S(2)}) collective-permute-start(bf16[1,16,7168]{2,1,0:T(8,128)(2,1)S(1)} %broadcast_select_fusion.5), channel_id=1, source_target_pairs={{8,0},{16,8},{24,16},{9,1},{17,9},{25,17},{10,2},{18,10},{26,18},{... | collective-permute-start | bytes 688136 | tf_op jit(solution)/shard_map/while/body/eval_jaxpr/ppermute | solution.py:17
  37.3 18.4 %all-to-all-start = ((bf16[8,10,3584]{2,1,0:T(8,128)(2,1)}), bf16[8,10,3584]{2,1,0:T(8,128)(2,1)S(1)}, u32[]{:S(2)}, u32[]{:S(2)}) async-start(bf16[8,10,3584]{2,1,0:T(8,128)(2,1)} %fusion.82), calls=%async_computation | async-start | bytes 1835008 | tf_op jit(solution)/shard_map/while/body/eval_jaxpr/all_to_all | solution.py:32
  59.7 9.5 %collective-permute-start.10 = (bf16[16,7168]{1,0:T(8,128)(2,1)S(1)}, bf16[16,7168]{1,0:T(8,128)(2,1)S(1)}, u32[]{:S(2)}, u32[]{:S(2)}) collective-permute-start(bf16[16,7168]{1,0:T(8,128)(2,1)S(1)} %get-tuple-element.539), channel_id=1, source_target_pairs={{0,8},{8,16},{16,24},{1,9},{9,17},{17,25},{2,10},{10,18},{18,26},{... | collective-permute-start | bytes 688136 | tf_op jit(solution)/shard_map/while/body/eval_jaxpr/ppermute | solution.py:17
  75.1 12.5 %collective-permute-start.4 = (bf16[1,10,3584]{2,1,0:T(8,128)(2,1)S(1)}, bf16[1,10,3584]{2,1,0:T(8,128)(2,1)S(1)}, u32[]{:S(2)}, u32[]{:S(2)}) collective-permute-start(bf16[1,10,3584]{2,1,0:T(8,128)(2,1)S(1)} %get-tuple-element.529), channel_id=1, source_target_pairs={{0,4},{1,5},{2,6},{3,7},{4,0},{5,1},{6,2},{7,3},{8,12},{9,13},{10,... | collective-permute-start | bytes 215048 | tf_op jit(solution)/shard_map/while/body/eval_jaxpr/ppermute | solution.py:85
  76.9 10.8 %collective-permute-start.5 = (bf16[1,10,3584]{2,1,0:T(8,128)(2,1)S(1)}, bf16[1,10,3584]{2,1,0:T(8,128)(2,1)S(1)}, u32[]{:S(2)}, u32[]{:S(2)}) collective-permute-start(bf16[1,10,3584]{2,1,0:T(8,128)(2,1)S(1)} %get-tuple-element.530), channel_id=1, source_target_pairs={{0,3},{1,4},{2,5},{3,6},{4,7},{5,0},{6,1},{7,2},{8,11},{9,12},{10,... | collective-permute-start | bytes 215048 | tf_op jit(solution)/shard_map/while/body/eval_jaxpr/ppermute | solution.py:85
  88.6 38.8 %collective-permute-start = (bf16[1,16,7168]{2,1,0:T(8,128)(2,1)S(1)}, bf16[1,16,7168]{2,1,0:T(8,128)(2,1)S(1)}, u32[]{:S(2)}, u32[]{:S(2)}) collective-permute-start(bf16[1,16,7168]{2,1,0:T(8,128)(2,1)S(1)} %broadcast_select_fusion.5), channel_id=1, source_target_pairs={{8,0},{16,8},{24,16},{9,1},{17,9},{25,17},{10,2},{18,10},{26,18},{... | collective-permute-start | bytes 688136 | tf_op jit(solution)/shard_map/while/body/eval_jaxpr/ppermute | solution.py:17
  105.6 17.9 %all-to-all-start = ((bf16[8,10,3584]{2,1,0:T(8,128)(2,1)}), bf16[8,10,3584]{2,1,0:T(8,128)(2,1)S(1)}, u32[]{:S(2)}, u32[]{:S(2)}) async-start(bf16[8,10,3584]{2,1,0:T(8,128)(2,1)} %fusion.82), calls=%async_computation | async-start | bytes 1835008 | tf_op jit(solution)/shard_map/while/body/eval_jaxpr/all_to_all | solution.py:32
  127.6 9.5 %collective-permute-start.10 = (bf16[16,7168]{1,0:T(8,128)(2,1)S(1)}, bf16[16,7168]{1,0:T(8,128)(2,1)S(1)}, u32[]{:S(2)}, u32[]{:S(2)}) collective-permute-start(bf16[16,7168]{1,0:T(8,128)(2,1)S(1)} %get-tuple-element.539), channel_id=1, source_target_pairs={{0,8},{8,16},{16,24},{1,9},{9,17},{17,25},{2,10},{10,18},{18,26},{... | collective-permute-start | bytes 688136 | tf_op jit(solution)/shard_map/while/body/eval_jaxpr/ppermute | solution.py:17
  143.0 12.5 %collective-permute-start.4 = (bf16[1,10,3584]{2,1,0:T(8,128)(2,1)S(1)}, bf16[1,10,3584]{2,1,0:T(8,128)(2,1)S(1)}, u32[]{:S(2)}, u32[]{:S(2)}) collective-permute-start(bf16[1,10,3584]{2,1,0:T(8,128)(2,1)S(1)} %get-tuple-element.529), channel_id=1, source_target_pairs={{0,4},{1,5},{2,6},{3,7},{4,0},{5,1},{6,2},{7,3},{8,12},{9,13},{10,... | collective-permute-start | bytes 215048 | tf_op jit(solution)/shard_map/while/body/eval_jaxpr/ppermute | solution.py:85
  144.8 10.8 %collective-permute-start.5 = (bf16[1,10,3584]{2,1,0:T(8,128)(2,1)S(1)}, bf16[1,10,3584]{2,1,0:T(8,128)(2,1)S(1)}, u32[]{:S(2)}, u32[]{:S(2)}) collective-permute-start(bf16[1,10,3584]{2,1,0:T(8,128)(2,1)S(1)} %get-tuple-element.530), channel_id=1, source_target_pairs={{0,3},{1,4},{2,5},{3,6},{4,7},{5,0},{6,1},{7,2},{8,11},{9,12},{10,... | collective-permute-start | bytes 215048 | tf_op jit(solution)/shard_map/while/body/eval_jaxpr/ppermute | solution.py:85
  156.5 38.8 %collective-permute-start = (bf16[1,16,7168]{2,1,0:T(8,128)(2,1)S(1)}, bf16[1,16,7168]{2,1,0:T(8,128)(2,1)S(1)}, u32[]{:S(2)}, u32[]{:S(2)}) collective-permute-start(bf16[1,16,7168]{2,1,0:T(8,128)(2,1)S(1)} %broadcast_select_fusion.5), channel_id=1, source_target_pairs={{8,0},{16,8},{24,16},{9,1},{17,9},{25,17},{10,2},{18,10},{26,18},{... | collective-permute-start | bytes 688136 | tf_op jit(solution)/shard_map/while/body/eval_jaxpr/ppermute | solution.py:17
  173.5 17.9 %all-to-all-start = ((bf16[8,10,3584]{2,1,0:T(8,128)(2,1)}), bf16[8,10,3584]{2,1,0:T(8,128)(2,1)S(1)}, u32[]{:S(2)}, u32[]{:S(2)}) async-start(bf16[8,10,3584]{2,1,0:T(8,128)(2,1)} %fusion.82), calls=%async_computation | async-start | bytes 1835008 | tf_op jit(solution)/shard_map/while/body/eval_jaxpr/all_to_all | solution.py:32
  195.5 9.5 %collective-permute-start.10 = (bf16[16,7168]{1,0:T(8,128)(2,1)S(1)}, bf16[16,7168]{1,0:T(8,128)(2,1)S(1)}, u32[]{:S(2)}, u32[]{:S(2)}) collective-permute-start(bf16[16,7168]{1,0:T(8,128)(2,1)S(1)} %get-tuple-element.539), channel_id=1, source_target_pairs={{0,8},{8,16},{16,24},{1,9},{9,17},{17,25},{2,10},{10,18},{18,26},{... | collective-permute-start | bytes 688136 | tf_op jit(solution)/shard_map/while/body/eval_jaxpr/ppermute | solution.py:17
  210.9 12.5 %collective-permute-start.4 = (bf16[1,10,3584]{2,1,0:T(8,128)(2,1)S(1)}, bf16[1,10,3584]{2,1,0:T(8,128)(2,1)S(1)}, u32[]{:S(2)}, u32[]{:S(2)}) collective-permute-start(bf16[1,10,3584]{2,1,0:T(8,128)(2,1)S(1)} %get-tuple-element.529), channel_id=1, source_target_pairs={{0,4},{1,5},{2,6},{3,7},{4,0},{5,1},{6,2},{7,3},{8,12},{9,13},{10,... | collective-permute-start | bytes 215048 | tf_op jit(solution)/shard_map/while/body/eval_jaxpr/ppermute | solution.py:85
  212.7 10.8 %collective-permute-start.5 = (bf16[1,10,3584]{2,1,0:T(8,128)(2,1)S(1)}, bf16[1,10,3584]{2,1,0:T(8,128)(2,1)S(1)}, u32[]{:S(2)}, u32[]{:S(2)}) collective-permute-start(bf16[1,10,3584]{2,1,0:T(8,128)(2,1)S(1)} %get-tuple-element.530), channel_id=1, source_target_pairs={{0,3},{1,4},{2,5},{3,6},{4,7},{5,0},{6,1},{7,2},{8,11},{9,12},{10,... | collective-permute-start | bytes 215048 | tf_op jit(solution)/shard_map/while/body/eval_jaxpr/ppermute | solution.py:85
  224.4 38.5 %collective-permute-start = (bf16[1,16,7168]{2,1,0:T(8,128)(2,1)S(1)}, bf16[1,16,7168]{2,1,0:T(8,128)(2,1)S(1)}, u32[]{:S(2)}, u32[]{:S(2)}) collective-permute-start(bf16[1,16,7168]{2,1,0:T(8,128)(2,1)S(1)} %broadcast_select_fusion.5), channel_id=1, source_target_pairs={{8,0},{16,8},{24,16},{9,1},{17,9},{25,17},{10,2},{18,10},{26,18},{... | collective-permute-start | bytes 688136 | tf_op jit(solution)/shard_map/while/body/eval_jaxpr/ppermute | solution.py:17
  241.1 17.9 %all-to-all-start = ((bf16[8,10,3584]{2,1,0:T(8,128)(2,1)}), bf16[8,10,3584]{2,1,0:T(8,128)(2,1)S(1)}, u32[]{:S(2)}, u32[]{:S(2)}) async-start(bf16[8,10,3584]{2,1,0:T(8,128)(2,1)} %fusion.82), calls=%async_computation | async-start | bytes 1835008 | tf_op jit(solution)/shard_map/while/body/eval_jaxpr/all_to_all | solution.py:32
  278.5 12.5 %collective-permute-start.4 = (bf16[1,10,3584]{2,1,0:T(8,128)(2,1)S(1)}, bf16[1,10,3584]{2,1,0:T(8,128)(2,1)S(1)}, u32[]{:S(2)}, u32[]{:S(2)}) collective-permute-start(bf16[1,10,3584]{2,1,0:T(8,128)(2,1)S(1)} %get-tuple-element.529), channel_id=1, source_target_pairs={{0,4},{1,5},{2,6},{3,7},{4,0},{5,1},{6,2},{7,3},{8,12},{9,13},{10,... | collective-permute-start | bytes 215048 | tf_op jit(solution)/shard_map/while/body/eval_jaxpr/ppermute | solution.py:85
  280.3 10.8 %collective-permute-start.5 = (bf16[1,10,3584]{2,1,0:T(8,128)(2,1)S(1)}, bf16[1,10,3584]{2,1,0:T(8,128)(2,1)S(1)}, u32[]{:S(2)}, u32[]{:S(2)}) collective-permute-start(bf16[1,10,3584]{2,1,0:T(8,128)(2,1)S(1)} %get-tuple-element.530), channel_id=1, source_target_pairs={{0,3},{1,4},{2,5},{3,6},{4,7},{5,0},{6,1},{7,2},{8,11},{9,12},{10,... | collective-permute-start | bytes 215048 | tf_op jit(solution)/shard_map/while/body/eval_jaxpr/ppermute | solution.py:85
  292.0 38.5 %collective-permute-start = (bf16[1,16,7168]{2,1,0:T(8,128)(2,1)S(1)}, bf16[1,16,7168]{2,1,0:T(8,128)(2,1)S(1)}, u32[]{:S(2)}, u32[]{:S(2)}) collective-permute-start(bf16[1,16,7168]{2,1,0:T(8,128)(2,1)S(1)} %broadcast_select_fusion.5), channel_id=1, source_target_pairs={{8,0},{16,8},{24,16},{9,1},{17,9},{25,17},{10,2},{18,10},{26,18},{... | collective-permute-start | bytes 688136 | tf_op jit(solution)/shard_map/while/body/eval_jaxpr/ppermute | solution.py:17
  308.7 17.9 %all-to-all-start = ((bf16[8,10,3584]{2,1,0:T(8,128)(2,1)}), bf16[8,10,3584]{2,1,0:T(8,128)(2,1)S(1)}, u32[]{:S(2)}, u32[]{:S(2)}) async-start(bf16[8,10,3584]{2,1,0:T(8,128)(2,1)} %fusion.82), calls=%async_computation | async-start | bytes 1835008 | tf_op jit(solution)/shard_map/while/body/eval_jaxpr/all_to_all | solution.py:32
  346.1 12.5 %collective-permute-start.4 = (bf16[1,10,3584]{2,1,0:T(8,128)(2,1)S(1)}, bf16[1,10,3584]{2,1,0:T(8,128)(2,1)S(1)}, u32[]{:S(2)}, u32[]{:S(2)}) collective-permute-start(bf16[1,10,3584]{2,1,0:T(8,128)(2,1)S(1)} %get-tuple-element.529), channel_id=1, source_target_pairs={{0,4},{1,5},{2,6},{3,7},{4,0},{5,1},{6,2},{7,3},{8,12},{9,13},{10,... | collective-permute-start | bytes 215048 | tf_op jit(solution)/shard_map/while/body/eval_jaxpr/ppermute | solution.py:85
  347.9 10.8 %collective-permute-start.5 = (bf16[1,10,3584]{2,1,0:T(8,128)(2,1)S(1)}, bf16[1,10,3584]{2,1,0:T(8,128)(2,1)S(1)}, u32[]{:S(2)}, u32[]{:S(2)}) collective-permute-start(bf16[1,10,3584]{2,1,0:T(8,128)(2,1)S(1)} %get-tuple-element.530), channel_id=1, source_target_pairs={{0,3},{1,4},{2,5},{3,6},{4,7},{5,0},{6,1},{7,2},{8,11},{9,12},{10,... | collective-permute-start | bytes 215048 | tf_op jit(solution)/shard_map/while/body/eval_jaxpr/ppermute | solution.py:85
  359.6 38.5 %collective-permute-start = (bf16[1,16,7168]{2,1,0:T(8,128)(2,1)S(1)}, bf16[1,16,7168]{2,1,0:T(8,128)(2,1)S(1)}, u32[]{:S(2)}, u32[]{:S(2)}) collective-permute-start(bf16[1,16,7168]{2,1,0:T(8,128)(2,1)S(1)} %broadcast_select_fusion.5), channel_id=1, source_target_pairs={{8,0},{16,8},{24,16},{9,1},{17,9},{25,17},{10,2},{18,10},{26,18},{... | collective-permute-start | bytes 688136 | tf_op jit(solution)/shard_map/while/body/eval_jaxpr/ppermute | solution.py:17
  376.3 17.9 %all-to-all-start = ((bf16[8,10,3584]{2,1,0:T(8,128)(2,1)}), bf16[8,10,3584]{2,1,0:T(8,128)(2,1)S(1)}, u32[]{:S(2)}, u32[]{:S(2)}) async-start(bf16[8,10,3584]{2,1,0:T(8,128)(2,1)} %fusion.82), calls=%async_computation | async-start | bytes 1835008 | tf_op jit(solution)/shard_map/while/body/eval_jaxpr/all_to_all | solution.py:32
  398.3 9.5 %collective-permute-start.10 = (bf16[16,7168]{1,0:T(8,128)(2,1)S(1)}, bf16[16,7168]{1,0:T(8,128)(2,1)S(1)}, u32[]{:S(2)}, u32[]{:S(2)}) collective-permute-start(bf16[16,7168]{1,0:T(8,128)(2,1)S(1)} %get-tuple-element.539), channel_id=1, source_target_pairs={{0,8},{8,16},{16,24},{1,9},{9,17},{17,25},{2,10},{10,18},{18,26},{... | collective-permute-start | bytes 688136 | tf_op jit(solution)/shard_map/while/body/eval_jaxpr/ppermute | solution.py:17
  413.7 12.5 %collective-permute-start.4 = (bf16[1,10,3584]{2,1,0:T(8,128)(2,1)S(1)}, bf16[1,10,3584]{2,1,0:T(8,128)(2,1)S(1)}, u32[]{:S(2)}, u32[]{:S(2)}) collective-permute-start(bf16[1,10,3584]{2,1,0:T(8,128)(2,1)S(1)} %get-tuple-element.529), channel_id=1, source_target_pairs={{0,4},{1,5},{2,6},{3,7},{4,0},{5,1},{6,2},{7,3},{8,12},{9,13},{10,... | collective-permute-start | bytes 215048 | tf_op jit(solution)/shard_map/while/body/eval_jaxpr/ppermute | solution.py:85
  415.5 10.8 %collective-permute-start.5 = (bf16[1,10,3584]{2,1,0:T(8,128)(2,1)S(1)}, bf16[1,10,3584]{2,1,0:T(8,128)(2,1)S(1)}, u32[]{:S(2)}, u32[]{:S(2)}) collective-permute-start(bf16[1,10,3584]{2,1,0:T(8,128)(2,1)S(1)} %get-tuple-element.530), channel_id=1, source_target_pairs={{0,3},{1,4},{2,5},{3,6},{4,7},{5,0},{6,1},{7,2},{8,11},{9,12},{10,... | collective-permute-start | bytes 215048 | tf_op jit(solution)/shard_map/while/body/eval_jaxpr/ppermute | solution.py:85
  427.3 38.5 %collective-permute-start = (bf16[1,16,7168]{2,1,0:T(8,128)(2,1)S(1)}, bf16[1,16,7168]{2,1,0:T(8,128)(2,1)S(1)}, u32[]{:S(2)}, u32[]{:S(2)}) collective-permute-start(bf16[1,16,7168]{2,1,0:T(8,128)(2,1)S(1)} %broadcast_select_fusion.5), channel_id=1, source_target_pairs={{8,0},{16,8},{24,16},{9,1},{17,9},{25,17},{10,2},{18,10},{26,18},{... | collective-permute-start | bytes 688136 | tf_op jit(solution)/shard_map/while/body/eval_jaxpr/ppermute | solution.py:17
  443.9 17.9 %all-to-all-start = ((bf16[8,10,3584]{2,1,0:T(8,128)(2,1)}), bf16[8,10,3584]{2,1,0:T(8,128)(2,1)S(1)}, u32[]{:S(2)}, u32[]{:S(2)}) async-start(bf16[8,10,3584]{2,1,0:T(8,128)(2,1)} %fusion.82), calls=%async_computation | async-start | bytes 1835008 | tf_op jit(solution)/shard_map/while/body/eval_jaxpr/all_to_all | solution.py:32
  (102 other events, 628.5 us)
